TPU v7x, 256 devices: a whole 4x4x8 slice. The times are simulated.
256 devices in a mesh: wide: 32 (over x, y, core), narrow: 8 (over z).
Axes of the slice: x: 4, y: 4, z: 8, core: 2. Of those that a mesh axis runs over, the one named last changes fastest.
Arguments:
- panels: float32 [256, 512, 512], P('wide', 'narrow'), may hold values from -0.6 to 0.6
- factors: float32 [64, 512, 512], P('wide', 'narrow'), may hold values from -2 to 2
- member: int32 [64, 4], replicated, may hold values from 0 to 255, as said below
- target: int32 [64, 10], replicated, may hold values from 0 to 31
- ancestors: float32 [32, 512, 512], P('wide', 'narrow'), may hold values from -6 to 6
Outputs:
- updated: float32 [32, 512, 512], P('wide', 'narrow')
Inputs may be any that keep to these rules, and one draw needn't show every extreme that they name: `member`: the blocks of supernode s are 4 distinct indices in [(s // 2) * 8, (s // 2 + 1) * 8); every block belongs to exactly one supernode.
All inputs are finite; a program needn't handle non-finite values.
Results may differ from a plain program's by a relative error of at most 0.0003.
Values sent between devices are 32-bit elements; how exact they have to be, the bound alone decides.
No kernel may reach another device: no remote copies, remote signals or barrier semaphores. Data moves between devices by JAX's collectives and lax.ppermute only.
A program may use at most 128 MiB of HBM per device.

v0:
```python
import jax
import jax.numpy as jnp
import numpy as np
from jax import lax
from jax.sharding import PartitionSpec as P


def pair_lists(count):
    left_pick = []
    right_pick = []
    for upper in range(count):
        for lower in range(upper + 1):
            left_pick.append(upper)
            right_pick.append(lower)
    return (np.array(left_pick, dtype=np.int32), np.array(right_pick, dtype=np.int32))


def shards(panels, factors, member, target, ancestors):
    highest = lax.Precision.HIGHEST
    sup_count = factors.shape[0]
    blk_count = panels.shape[0]
    tile_count = ancestors.shape[0] * lax.axis_size("wide")
    left_pick, right_pick = pair_lists(member.shape[1])
    owner_index = lax.axis_index("wide")
    own_members = (
        lax.dynamic_slice_in_dim(member, owner_index * sup_count, sup_count, 0)
        - owner_index * blk_count
    )
    own_targets = lax.dynamic_slice_in_dim(target, owner_index * sup_count, sup_count, 0)
    full_factors = lax.all_gather(factors, "narrow", axis=1, tiled=True)
    blocks = panels[own_members]
    scaled = jnp.einsum("skrw,swv->skrv", blocks, full_factors, precision=highest)
    left_rows = scaled[:, left_pick]
    right_rows = lax.all_gather(scaled, "narrow", axis=2, tiled=True)[:, right_pick]
    updates = jnp.einsum("sprv,spmv->sprm", left_rows, right_rows, precision=highest)
    tile_ids = jnp.arange(tile_count, dtype=jnp.int32)
    onehot = (own_targets[:, :, None] == tile_ids[None, None, :]).astype(jnp.float32)
    portion = jnp.einsum("spa,sprw->arw", onehot, updates, precision=highest)
    totals = lax.psum_scatter(portion, "wide", scatter_dimension=0, tiled=True)
    return ancestors - totals


def solution(mesh):
    return jax.shard_map(
        shards,
        mesh=mesh,
        in_specs=(
            P("wide", "narrow", None),
            P("wide", "narrow", None),
            P(),
            P(),
            P("wide", "narrow", None),
        ),
        out_specs=P("wide", "narrow", None),
        check_vma=False,
    )
```

profile of v0, /device:TPU:2, one launch (start us, length us, event | category | flops | bytes accessed | tf_op | source)
XLA Modules:
  0.0 293.5 jit_solution(6393277430765025806)
XLA Ops:
  6.5 0.0 copy-start
  6.5 0.0 all-gather.3.cloned.1.call-start
  6.5 0.7 all-gather.3.cloned.1.call-update
  7.3 0.0 all-gather.5.cloned.1.call-start
  7.3 0.8 compare_select_fusion
  8.1 0.1 copy.15
  8.2 0.1 reshape.3
  8.3 0.0 copy-done
  8.3 0.6 gather_fusion
  8.9 44.1 %all-gather.3.cloned.1.call-done = f32[2,512,512]{2,1,0:T(8,128)} async-done(((f32[2,64,512]{2,1,0:T(8,128)}), f32[2,512,512]{2,1,0:T(8,128)}) %all-gather.3.cloned.1.call-update) | async-done | bytes 2097168 | tf_op jit(solution)/shard_map/all_gather | solution.py:30
  53.0 0.0 copy-start.3
  53.0 0.0 copy-start.5
  53.0 0.0 copy-start.4
  53.0 4.5 %fusion.8 = f32[2,4,64,512]{3,2,1,0:T(8,128)} fusion(f32[2,4,64,512]{3,2,1,0:T(8,128)S(1)} %bitcast.21, f32[2,512,512]{2,1,0:T(8,128)} %all-gather.3.cloned.1.call-done), kind=kOutput, calls=%fused_computation.9 | convolution fusion | flops 1610612736 | bytes 4194304 | tf_op jit(solution)/shard_map/skrw,swv->skrv/dot_general | solution.py:32
  57.5 0.0 copy-start.1
  57.5 0.0 all-gather.5.cloned.1.call-update
  57.6 0.0 reduce-scatter.2.cloned.1.call-start
  57.6 0.0 copy-done.3
  57.6 0.1 constant_dynamic-slice_fusion
  57.7 0.1 copy.14
  57.8 0.0 copy-done.5
  57.8 0.0 copy-done.4
  57.8 0.9 copy-done.1
  58.8 2.2 gather_fusion.1
  60.9 89.4 %all-gather.5.cloned.1.call-done = f32[2,4,512,512]{3,2,1,0:T(8,128)} async-done(((f32[2,4,64,512]{3,2,1,0:T(8,128)}), f32[2,4,512,512]{3,2,1,0:T(8,128)}) %all-gather.5.cloned.1.call-update) | async-done | bytes 8388624 | tf_op jit(solution)/shard_map/all_gather | solution.py:34
  150.3 12.6 %gather_fusion.2 = f32[10,2,512,512]{3,2,1,0:T(8,128)} fusion(f32[2,4,512,512]{3,2,1,0:T(8,128)} %all-gather.5.cloned.1.call-done, s32[1024]{0:T(1024)S(1)} %pad_clamp_fusion), kind=kCustom, calls=%fused_computation.2 | custom fusion | bytes 41943080 | tf_op jit(solution)/shard_map/gather | solution.py:34
  162.9 25.8 %fusion = f32[2,10,64,512]{3,2,1,0:T(8,128)S(1)} fusion(f32[10,2,512,512]{3,2,1,0:T(8,128)} %gather_fusion.2, f32[10,2,64,512]{3,2,1,0:T(8,128)} %gather_fusion.1), kind=kOutput, calls=%fused_computation.3 | convolution fusion | flops 4026531840 | bytes 26214400 | tf_op jit(solution)/shard_map/sprv,spmv->sprm/dot_general | solution.py:35
  188.7 3.9 %fusion.5 = f32[32,64,512]{2,0,1:T(8,128)S(1)} fusion(f32[2,10,64,512]{3,2,1,0:T(8,128)S(1)} %fusion, s32[2,10]{1,0:T(2,128)S(1)} %copy.14), kind=kOutput, calls=%fused_computation.8 | convolution fusion | flops 251658880 | bytes 6815824 | tf_op jit(solution)/shard_map/spa,sprw->arw/dot_general | solution.py:38
  192.6 4.4 %copy.16 = f32[32,64,512]{2,1,0:T(8,128)} copy(f32[32,64,512]{2,0,1:T(8,128)S(1)} %fusion.5) | data formatting | bytes 8388608 | tf_op jit(solution)/shard_map/spa,sprw->arw/dot_general | solution.py:38
  197.0 0.0 copy-start.2
  197.0 0.0 reduce-scatter.2.cloned.1.call-update
  197.0 88.4 %reduce-scatter.2.cloned.1.call-done = f32[1,64,512]{2,1,0:T(8,128)} async-done(((f32[32,64,512]{2,1,0:T(8,128)}), f32[1,64,512]{2,1,0:T(8,128)}) %reduce-scatter.2.cloned.1.call-update) | async-done | bytes 131088 | tf_op jit(solution)/shard_map/reduce_scatter | solution.py:39
  285.4 0.0 copy-done.2
  285.4 1.6 sub.11
  (3 shorter events, 0.0 us)
Async XLA Ops:
  6.5 1.7 copy-start
  6.5 46.4 %all-gather.3.cloned.1.call-start = ((), (), s32[]{:S(2)}) async-start(), calls=%async_computation.1 | async-start | bytes 2359296 | tf_op jit(solution)/shard_map/all_gather | solution.py:30
  7.3 143.1 %all-gather.5.cloned.1.call-start = ((), (), s32[]{:S(2)}) async-start(), calls=%async_computation.2 | async-start | bytes 9437184 | tf_op jit(solution)/shard_map/all_gather | solution.py:34
  53.0 4.6 %copy-start.3 = (s32[64,10]{0,1:T(8,128)S(1)}, s32[64,10]{0,1:T(8,128)}, u32[]{:S(2)}) copy-start(s32[64,10]{0,1:T(8,128)} %param.12) | copy-start | bytes 7684
  53.0 4.8 %copy-start.5 = (s32[10]{0:T(128)S(1)}, s32[10]{0:T(128)}, u32[]{:S(2)}) copy-start(s32[10]{0:T(128)} %constant.33) | copy-start | bytes 124
  53.0 4.8 %copy-start.4 = (s32[10]{0:T(128)S(1)}, s32[10]{0:T(128)}, u32[]{:S(2)}) copy-start(s32[10]{0:T(128)} %constant.32) | copy-start | bytes 124
  57.5 1.2 copy-start.1
  57.6 227.9 %reduce-scatter.2.cloned.1.call-start = ((), (), s32[]{:S(2)}) async-start(), calls=%async_computation.3 | async-start | bytes 4325376 | tf_op jit(solution)/shard_map/reduce_scatter | solution.py:39
  197.0 88.4 %copy-start.2 = (f32[1,64,512]{2,1,0:T(8,128)S(1)}, f32[1,64,512]{2,1,0:T(8,128)}, u32[]{:S(2)}) copy-start(f32[1,64,512]{2,1,0:T(8,128)} %param.13) | copy-start | bytes 393220
Sparse Core Ops, SparseCore 0:
  9.1 43.8 all-gather.2
  57.7 92.6 all-gather.4
  197.1 88.2 reduce-scatter.1
where the time goes:
time: 294 us
  waiting for transfers between devices  223 us (76%)
  matrix products  34.2 us (12%)
  local copies, waits for them, and re-layouts  21.1 us (7%)
  between operations  13.2 us (4%)
    all_gather x1, waiting for transfers between devices, shards(): lax.all_gather(scaled, 'narrow', axis=2, tiled=True)[:, right_pick]  89.4 us
    reduce_scatter x1, waiting for transfers between devices, shards(): totals = lax.psum_scatter(portion, 'wide', scatter_dimension=0, tiled=True)  88.4 us
    all_gather x1, waiting for transfers between devices, shards(): full_factors = lax.all_gather(factors, 'narrow', axis=1, tiled=True)  44.1 us
    dot_general x1, matrix products, shards(): jnp.einsum('sprv,spmv->sprm', left_rows, right_rows, precision=highest)  25.8 us
    gather x1, local copies, waits for them, and re-layouts, shards(): lax.all_gather(scaled, 'narrow', axis=2, tiled=True)[:, right_pick]  12.6 us
  transfers between devices with their start and end apart: 3, of which 3 were waited for; matrix products, arithmetic and copies ran while one was open for 1% of the time, Pallas kernels for 0%

commit v1 on v0

--- a/solution.py
+++ b/solution.py
@@ -3,6 +3,27 @@
 import numpy as np
 from jax import lax
 from jax.sharding import PartitionSpec as P
+
+
+def collect(value, axis, dim):
+    size, place, width = (lax.axis_size(axis), lax.axis_index(axis), value.shape[dim])
+    right = [(i, (i + 1) % size) for i in range(size)]
+    backward = [(i, (i - 1) % size) for i in range(size)]
+    out = jnp.zeros((*value.shape[:dim], size * width, *value.shape[dim + 1 :]), value.dtype)
+    out = lax.dynamic_update_slice_in_dim(out, value, place * width, axis=dim)
+    from_left = from_right = value
+    halfway = size // 2
+    for turn in range(1, halfway + 1):
+        from_left = lax.ppermute(from_left, axis, right)
+        out = lax.dynamic_update_slice_in_dim(
+            out, from_left, (place - turn) % size * width, axis=dim
+        )
+        if turn < size - halfway:
+            from_right = lax.ppermute(from_right, axis, backward)
+            out = lax.dynamic_update_slice_in_dim(
+                out, from_right, (place + turn) % size * width, axis=dim
+            )
+    return out
 
 
 def pair_lists(count):
@@ -27,7 +48,7 @@
         - owner_index * blk_count
     )
     own_targets = lax.dynamic_slice_in_dim(target, owner_index * sup_count, sup_count, 0)
-    full_factors = lax.all_gather(factors, "narrow", axis=1, tiled=True)
+    full_factors = collect(factors, "narrow", 1)
     blocks = panels[own_members]
     scaled = jnp.einsum("skrw,swv->skrv", blocks, full_factors, precision=highest)
     left_rows = scaled[:, left_pick]

time: 294 us -> 284 us (0.966)
  waiting for transfers between devices: 223 us -> 196 us
  starting transfers between devices: 0.08 us -> 13.2 us
  local copies, waits for them, and re-layouts: 21.1 us -> 26.1 us
    all_gather x1 -> x0, waiting for transfers between devices: 44.1 us -> none  [shards(): full_factors = lax.all_gather(factors, 'narrow', axis=1, tiled=True)]
    ppermute x0 -> x7, waiting for transfers between devices: none -> 17.3 us  [the longest x4 16.9 us: collect(): from_left = lax.ppermute(from_left, axis, right)]
    ppermute x0 -> x7, starting transfers between devices: none -> 13 us  [the longest x3 11 us: collect(): from_right = lax.ppermute(from_right, axis, backward)]
    dynamic_update_slice x0 -> x8, local copies, waits for them, and re-layouts: none -> 3.97 us  [the longest x4 1.98 us: collect(): lax.dynamic_update_slice_in_dim(out, from_left, (place - turn) % size * w...]
  transfers between devices with their start and end apart: 3 -> 9, of which waited for: 3 -> 8; matrix products, arithmetic and copies ran while one was open for 1% -> 3% of each run, Pallas kernels for 0% -> 0%
where the time goes in v1:
time: 284 us
  waiting for transfers between devices  196 us (69%)
  matrix products  32.6 us (11%)
  local copies, waits for them, and re-layouts  26.1 us (9%)
  between operations  13.5 us (5%)
  starting transfers between devices  13.2 us (5%)
    all_gather x1, waiting for transfers between devices, shards(): lax.all_gather(scaled, 'narrow', axis=2, tiled=True)[:, right_pick]  90.4 us
    reduce_scatter x1, waiting for transfers between devices, shards(): totals = lax.psum_scatter(portion, 'wide', scatter_dimension=0, tiled=True)  88.4 us
    dot_general x1, matrix products, shards(): jnp.einsum('sprv,spmv->sprm', left_rows, right_rows, precision=highest)  25.8 us
    ppermute x4, waiting for transfers between devices, collect(): from_left = lax.ppermute(from_left, axis, right)  16.9 us
    gather x1, local copies, waits for them, and re-layouts, shards(): lax.all_gather(scaled, 'narrow', axis=2, tiled=True)[:, right_pick]  12.6 us
    ppermute x3, starting transfers between devices, collect(): from_right = lax.ppermute(from_right, axis, backward)  11 us
  transfers between devices with their start and end apart: 9, of which 8 were waited for; matrix products, arithmetic and copies ran while one was open for 3% of the time, Pallas kernels for 0%

profile of v1, /device:TPU:2, one launch (start us, length us, event | category | flops | bytes accessed | tf_op | source)
XLA Modules:
  0.0 284.0 jit_solution(9113508424395784928)
XLA Ops:
  6.5 0.0 copy-start
  6.5 0.0 all-gather.2.cloned.1.call-start
  6.5 1.9 collective-permute-start
  8.5 3.9 %collective-permute-start.1 = (f32[2,64,512]{2,1,0:T(8,128)}, f32[2,64,512]{2,1,0:T(8,128)S(1)}, u32[]{:S(2)}, u32[]{:S(2)}) collective-permute-start(f32[2,64,512]{2,1,0:T(8,128)} %param.10), channel_id=1, source_target_pairs={{0,7},{1,0},{2,1},{3,2},{4,3},{5,4},{6,5},{7,6},{8,15},{9,8},{10,9... | collective-permute-start | bytes 786440 | tf_op jit(solution)/shard_map/ppermute | solution.py:22
  12.4 6.6 %collective-permute-done = f32[2,64,512]{2,1,0:T(8,128)} collective-permute-done((f32[2,64,512]{2,1,0:T(8,128)}, f32[2,64,512]{2,1,0:T(8,128)}, u32[]{:S(2)}, u32[]{:S(2)}) %collective-permute-start) | collective-permute-done | bytes 262176 | tf_op jit(solution)/shard_map/ppermute | solution.py:17
  19.0 0.0 collective-permute-start.2
  19.0 0.8 compare_select_fusion
  19.8 0.1 copy.15
  19.9 0.1 reshape.3
  20.0 0.2 broadcast_in_dim.15
  20.2 1.0 constant_dynamic-update-slice_fusion.7
  21.2 0.0 collective-permute-done.1
  21.2 3.3 %collective-permute-start.3 = (f32[2,64,512]{2,1,0:T(8,128)S(1)}, f32[2,64,512]{2,1,0:T(8,128)}, u32[]{:S(2)}, u32[]{:S(2)}) collective-permute-start(f32[2,64,512]{2,1,0:T(8,128)S(1)} %collective-permute-done.1), channel_id=1, source_target_pairs={{0,7},{1,0},{2,1},{3,2},{4,3},{5,4},{6,5},{7,6},{8,15},{9,8},{10,9... | collective-permute-start | bytes 786440 | tf_op jit(solution)/shard_map/ppermute | solution.py:22
  24.5 0.0 copy-done
  24.5 1.6 gather_fusion
  26.1 1.9 collective-permute-done.2
  28.0 0.0 collective-permute-start.4
  28.0 1.0 constant_dynamic-update-slice_fusion.6
  29.0 0.2 collective-permute-done.3
  29.2 3.8 %collective-permute-start.5 = (f32[2,64,512]{2,1,0:T(8,128)}, f32[2,64,512]{2,1,0:T(8,128)S(1)}, u32[]{:S(2)}, u32[]{:S(2)}) collective-permute-start(f32[2,64,512]{2,1,0:T(8,128)} %collective-permute-done.3), channel_id=1, source_target_pairs={{0,7},{1,0},{2,1},{3,2},{4,3},{5,4},{6,5},{7,6},{8,15},{9,8},{10,9... | collective-permute-start | bytes 786440 | tf_op jit(solution)/shard_map/ppermute | solution.py:22
  33.0 1.0 constant_dynamic-update-slice_fusion.4
  34.0 2.1 collective-permute-done.4
  36.0 0.0 collective-permute-start.6
  36.1 1.0 constant_dynamic-update-slice_fusion.3
  37.1 0.2 collective-permute-done.5
  37.3 6.4 %collective-permute-done.6 = f32[2,64,512]{2,1,0:T(8,128)S(1)} collective-permute-done((f32[2,64,512]{2,1,0:T(8,128)S(1)}, f32[2,64,512]{2,1,0:T(8,128)S(1)}, u32[]{:S(2)}, u32[]{:S(2)}) %collective-permute-start.6) | collective-permute-done | bytes 262176 | tf_op jit(solution)/shard_map/ppermute | solution.py:17
  43.7 0.0 copy-done.2
  43.7 0.0 copy-start.4
  43.7 0.0 copy-start.6
  43.7 0.0 copy-start.5
  43.7 2.9 %fusion.8 = f32[2,4,64,512]{3,2,1,0:T(8,128)} fusion(f32[2,4,64,512]{3,2,1,0:T(8,128)S(1)} %bitcast.21, f32[2,512,512]{2,1,0:T(8,128)S(1)} %constant_dynamic-update-slice_fusion), kind=kOutput, calls=%fused_computation.9 | convolution fusion | flops 1610612736 | bytes 4194304 | tf_op jit(solution)/shard_map/skrw,swv->skrv/dot_general | solution.py:53
  46.6 0.0 all-gather.2.cloned.1.call-update
  46.7 0.2 reduce-scatter.2.cloned.1.call-start
  46.9 0.0 copy-done.4
  46.9 0.1 constant_dynamic-slice_fusion.1
  47.0 0.1 copy.14
  47.1 0.0 copy-done.6
  47.1 0.8 copy-done.1
  47.9 2.2 gather_fusion.1
  50.0 90.4 %all-gather.2.cloned.1.call-done = f32[2,4,512,512]{3,2,1,0:T(8,128)} async-done(((f32[2,4,64,512]{3,2,1,0:T(8,128)}), f32[2,4,512,512]{3,2,1,0:T(8,128)}) %all-gather.2.cloned.1.call-update) | async-done | bytes 8388624 | tf_op jit(solution)/shard_map/all_gather | solution.py:55
  140.4 12.6 %gather_fusion.2 = f32[10,2,512,512]{3,2,1,0:T(8,128)} fusion(f32[2,4,512,512]{3,2,1,0:T(8,128)} %all-gather.2.cloned.1.call-done, s32[1024]{0:T(1024)S(1)} %pad_clamp_fusion), kind=kCustom, calls=%fused_computation.2 | custom fusion | bytes 41943080 | tf_op jit(solution)/shard_map/gather | solution.py:55
  153.0 25.8 %fusion = f32[2,10,64,512]{3,2,1,0:T(8,128)S(1)} fusion(f32[10,2,512,512]{3,2,1,0:T(8,128)} %gather_fusion.2, f32[10,2,64,512]{3,2,1,0:T(8,128)} %gather_fusion.1), kind=kOutput, calls=%fused_computation.3 | convolution fusion | flops 4026531840 | bytes 26214400 | tf_op jit(solution)/shard_map/sprv,spmv->sprm/dot_general | solution.py:56
  178.8 3.9 %fusion.5 = f32[32,64,512]{2,0,1:T(8,128)S(1)} fusion(f32[2,10,64,512]{3,2,1,0:T(8,128)S(1)} %fusion, s32[2,10]{1,0:T(2,128)S(1)} %copy.14), kind=kOutput, calls=%fused_computation.8 | convolution fusion | flops 251658880 | bytes 6815824 | tf_op jit(solution)/shard_map/spa,sprw->arw/dot_general | solution.py:59
  182.7 4.4 %copy.16 = f32[32,64,512]{2,1,0:T(8,128)} copy(f32[32,64,512]{2,0,1:T(8,128)S(1)} %fusion.5) | data formatting | bytes 8388608 | tf_op jit(solution)/shard_map/spa,sprw->arw/dot_general | solution.py:59
  187.1 0.0 reduce-scatter.2.cloned.1.call-update
  187.1 88.4 %reduce-scatter.2.cloned.1.call-done = f32[1,64,512]{2,1,0:T(8,128)} async-done(((f32[32,64,512]{2,1,0:T(8,128)}), f32[1,64,512]{2,1,0:T(8,128)}) %reduce-scatter.2.cloned.1.call-update) | async-done | bytes 131088 | tf_op jit(solution)/shard_map/reduce_scatter | solution.py:60
  275.6 0.0 copy-done.3
  275.6 1.6 sub.27
  (11 shorter events, 0.1 us)
Async XLA Ops:
  6.5 18.0 %copy-start = (f32[8,64,512]{2,1,0:T(8,128)S(1)}, f32[8,64,512]{2,1,0:T(8,128)}, u32[]{:S(2)}) copy-start(f32[8,64,512]{2,1,0:T(8,128)} %param.9) | copy-start | bytes 3145732
  6.5 133.9 %all-gather.2.cloned.1.call-start = ((), (), s32[]{:S(2)}) async-start(), calls=%async_computation.1 | async-start | bytes 9437184 | tf_op jit(solution)/shard_map/all_gather | solution.py:55
  6.5 12.5 %collective-permute-start = (f32[2,64,512]{2,1,0:T(8,128)}, f32[2,64,512]{2,1,0:T(8,128)}, u32[]{:S(2)}, u32[]{:S(2)}) collective-permute-start(f32[2,64,512]{2,1,0:T(8,128)} %param.10), channel_id=1, source_target_pairs={{0,1},{1,2},{2,3},{3,4},{4,5},{5,6},{6,7},{7,0},{8,9},{9,10},{10,1... | collective-permute-start | bytes 786440 | tf_op jit(solution)/shard_map/ppermute | solution.py:17
  8.5 12.7 %collective-permute-start.1 = (f32[2,64,512]{2,1,0:T(8,128)}, f32[2,64,512]{2,1,0:T(8,128)S(1)}, u32[]{:S(2)}, u32[]{:S(2)}) collective-permute-start(f32[2,64,512]{2,1,0:T(8,128)} %param.10), channel_id=1, source_target_pairs={{0,7},{1,0},{2,1},{3,2},{4,3},{5,4},{6,5},{7,6},{8,15},{9,8},{10,9... | collective-permute-start | bytes 786440 | tf_op jit(solution)/shard_map/ppermute | solution.py:22
  19.0 9.0 %collective-permute-start.2 = (f32[2,64,512]{2,1,0:T(8,128)}, f32[2,64,512]{2,1,0:T(8,128)}, u32[]{:S(2)}, u32[]{:S(2)}) collective-permute-start(f32[2,64,512]{2,1,0:T(8,128)} %collective-permute-done), channel_id=1, source_target_pairs={{0,1},{1,2},{2,3},{3,4},{4,5},{5,6},{6,7},{7,0},{8,9},{9,10},{10,1... | collective-permute-start | bytes 786440 | tf_op jit(solution)/shard_map/ppermute | solution.py:17
  21.2 8.0 %collective-permute-start.3 = (f32[2,64,512]{2,1,0:T(8,128)S(1)}, f32[2,64,512]{2,1,0:T(8,128)}, u32[]{:S(2)}, u32[]{:S(2)}) collective-permute-start(f32[2,64,512]{2,1,0:T(8,128)S(1)} %collective-permute-done.1), channel_id=1, source_target_pairs={{0,7},{1,0},{2,1},{3,2},{4,3},{5,4},{6,5},{7,6},{8,15},{9,8},{10,9... | collective-permute-start | bytes 786440 | tf_op jit(solution)/shard_map/ppermute | solution.py:22
  26.1 17.5 %copy-start.2 = (f32[8,64,512]{2,1,0:T(8,128)S(1)}, f32[8,64,512]{2,1,0:T(8,128)}, u32[]{:S(2)}) copy-start(f32[8,64,512]{2,1,0:T(8,128)} %gather_fusion) | copy-start | bytes 3145732
  28.0 8.0 %collective-permute-start.4 = (f32[2,64,512]{2,1,0:T(8,128)}, f32[2,64,512]{2,1,0:T(8,128)S(1)}, u32[]{:S(2)}, u32[]{:S(2)}) collective-permute-start(f32[2,64,512]{2,1,0:T(8,128)} %collective-permute-done.2), channel_id=1, source_target_pairs={{0,1},{1,2},{2,3},{3,4},{4,5},{5,6},{6,7},{7,0},{8,9},{9,10},{10,1... | collective-permute-start | bytes 786440 | tf_op jit(solution)/shard_map/ppermute | solution.py:17
  29.2 8.0 %collective-permute-start.5 = (f32[2,64,512]{2,1,0:T(8,128)}, f32[2,64,512]{2,1,0:T(8,128)S(1)}, u32[]{:S(2)}, u32[]{:S(2)}) collective-permute-start(f32[2,64,512]{2,1,0:T(8,128)} %collective-permute-done.3), channel_id=1, source_target_pairs={{0,7},{1,0},{2,1},{3,2},{4,3},{5,4},{6,5},{7,6},{8,15},{9,8},{10,9... | collective-permute-start | bytes 786440 | tf_op jit(solution)/shard_map/ppermute | solution.py:22
  36.0 7.6 %collective-permute-start.6 = (f32[2,64,512]{2,1,0:T(8,128)S(1)}, f32[2,64,512]{2,1,0:T(8,128)S(1)}, u32[]{:S(2)}, u32[]{:S(2)}) collective-permute-start(f32[2,64,512]{2,1,0:T(8,128)S(1)} %collective-permute-done.4), channel_id=1, source_target_pairs={{0,1},{1,2},{2,3},{3,4},{4,5},{5,6},{6,7},{7,0},{8,9},{9,10},{10,1... | collective-permute-start | bytes 786440 | tf_op jit(solution)/shard_map/ppermute | solution.py:17
  43.7 3.2 %copy-start.4 = (s32[64,10]{0,1:T(8,128)S(1)}, s32[64,10]{0,1:T(8,128)}, u32[]{:S(2)}) copy-start(s32[64,10]{0,1:T(8,128)} %param.12) | copy-start | bytes 7684
  43.7 3.4 %copy-start.6 = (s32[10]{0:T(128)S(1)}, s32[10]{0:T(128)}, u32[]{:S(2)}) copy-start(s32[10]{0:T(128)} %constant.87) | copy-start | bytes 124
  43.7 3.4 %copy-start.5 = (s32[10]{0:T(128)S(1)}, s32[10]{0:T(128)}, u32[]{:S(2)}) copy-start(s32[10]{0:T(128)} %constant.86) | copy-start | bytes 124
  46.6 1.2 copy-start.1
  46.7 228.9 %reduce-scatter.2.cloned.1.call-start = ((), (), s32[]{:S(2)}) async-start(), calls=%async_computation.2 | async-start | bytes 4325376 | tf_op jit(solution)/shard_map/reduce_scatter | solution.py:60
  187.1 88.4 %copy-start.3 = (f32[1,64,512]{2,1,0:T(8,128)S(1)}, f32[1,64,512]{2,1,0:T(8,128)}, u32[]{:S(2)}) copy-start(f32[1,64,512]{2,1,0:T(8,128)} %param.13) | copy-start | bytes 393220
Sparse Core Ops, SparseCore 0:
  46.8 93.5 all-gather.1
  187.3 88.2 reduce-scatter.1
